TPU v7x, 256 devices: a whole 4x4x8 slice. The times are simulated.
256 devices in a mesh: wide: 64 (over y, z, core), leaf: 4 (over x).
Axes of the slice: x: 4, y: 4, z: 8, core: 2. Of those that a mesh axis runs over, the one named last changes fastest.
Arguments:
- leaf_maps: float32 [64, 4, 2, 2, 512, 512], P('wide', 'leaf'), may hold values from -0.36 to 1.01
- angles: float32 [32], replicated, may hold values from -1.2 to 1.2
Outputs:
- reflected: float32 [64, 2, 64, 512], P('wide', None, 'leaf')
- transmitted: float32 [64, 2, 64, 512], P('wide', None, 'leaf')
All inputs are finite; a program needn't handle non-finite values.
Results may differ from a plain program's by a relative error of at most 0.0003.
Values sent between devices are 32-bit elements; how exact they have to be, the bound alone decides.
A program may use at most 320 MiB of HBM per device.

v0:
```python
import jax
import jax.numpy as jnp
from jax import lax
from jax.sharding import PartitionSpec as P

precise = lax.Precision.HIGHEST
wavenumber = 12.0


def from_partner(x, axis, apart):
    return lax.ppermute(x, axis, [(i, i ^ 1 << apart) for i in range(lax.axis_size(axis))])


def passed_along(x, axis, by):
    peers = lax.axis_size(axis)
    pairs = [(i, i + by) for i in range(peers) if 0 <= i + by < peers]
    return lax.ppermute(x, axis, pairs)


def plain_dot(left_mat, right_mat):
    return jnp.dot(left_mat, right_mat, precision=precise, preferred_element_type=jnp.float32)


def complex_dot(left_mat, right_mat):
    real_part = plain_dot(left_mat[0], right_mat[0]) - plain_dot(left_mat[1], right_mat[1])
    imag_part = plain_dot(left_mat[0], right_mat[1]) + plain_dot(left_mat[1], right_mat[0])
    return jnp.stack([real_part, imag_part])


def side_dot(vectors, matrix):
    return lax.dot_general(
        vectors,
        matrix,
        (((1,), (1,)), ((), ())),
        precision=precise,
        preferred_element_type=jnp.float32,
    )


def complex_apply(matrix, vectors):
    real_part = side_dot(vectors[0], matrix[0]) - side_dot(vectors[1], matrix[1])
    imag_part = side_dot(vectors[0], matrix[1]) + side_dot(vectors[1], matrix[0])
    return jnp.stack([real_part, imag_part])


def complex_solve(system, right_mat):
    size_n = system.shape[1]
    upper_band = jnp.concatenate([system[0], -system[1]], 1)
    lower_band = jnp.concatenate([system[1], system[0]], 1)
    big_mat = jnp.concatenate([upper_band, lower_band], 0)
    stacked = jnp.concatenate([right_mat[0], right_mat[1]], 0)
    normal = lax.dot_general(
        big_mat,
        big_mat,
        (((0,), (0,)), ((), ())),
        precision=precise,
        preferred_element_type=jnp.float32,
    )
    projected = lax.dot_general(
        big_mat,
        stacked,
        (((0,), (0,)), ((), ())),
        precision=precise,
        preferred_element_type=jnp.float32,
    )
    factor = jnp.linalg.cholesky(normal)
    solution = jax.scipy.linalg.cho_solve((factor, True), projected)
    return jnp.stack([solution[:size_n], solution[size_n:]])


def block_take(matrix, row_list, col_list):
    row_cat = jnp.concatenate([matrix[:, start_at:stop_at] for start_at, stop_at in row_list], 1)
    return jnp.concatenate([row_cat[:, :, start_at:stop_at] for start_at, stop_at in col_list], 2)


def merge_setup(map_lower, map_upper, side_pts, edge_pts, keeping):
    total_pts = 2 * side_pts + 2 * edge_pts
    lower_ext = 2 * side_pts + (edge_pts if keeping else 0)
    lower_outer = [(0, lower_ext)]
    lower_inner = [(2 * side_pts + edge_pts, total_pts)]
    upper_outer = [(0, 2 * side_pts)] + ([(2 * side_pts + edge_pts, total_pts)] if keeping else [])
    upper_inner = [(2 * side_pts, 2 * side_pts + edge_pts)]
    alpha_outer = block_take(map_lower, lower_outer, lower_outer)
    alpha_reach = block_take(map_lower, lower_outer, lower_inner)
    alpha_inward = block_take(map_lower, lower_inner, lower_outer)
    alpha_inner = block_take(map_lower, lower_inner, lower_inner)
    beta_outer = block_take(map_upper, upper_outer, upper_outer)
    beta_reach = block_take(map_upper, upper_outer, upper_inner)
    beta_inward = block_take(map_upper, upper_inner, upper_outer)
    beta_inner = block_take(map_upper, upper_inner, upper_inner)
    identity_mat = jnp.stack(
        [jnp.eye(edge_pts, dtype=jnp.float32), jnp.zeros((edge_pts, edge_pts), jnp.float32)]
    )
    system = identity_mat - complex_dot(beta_inner, alpha_inner)
    right_mat = jnp.concatenate([-complex_dot(beta_inner, alpha_inward), beta_inward], 2)
    solved = complex_solve(system, right_mat)
    blocks = (alpha_outer, alpha_reach, alpha_inward, alpha_inner, beta_outer, beta_reach)
    return (blocks, solved)


def rows_lower(blocks, solved):
    alpha_outer, alpha_reach = (blocks[0], blocks[1])
    upper_count = solved.shape[2] - alpha_outer.shape[2]
    padded = jnp.concatenate(
        [alpha_outer, jnp.zeros((2, alpha_outer.shape[1], upper_count), jnp.float32)], 2
    )
    return padded - complex_dot(alpha_reach, solved)


def rows_upper(blocks, solved):
    alpha_inward, alpha_inner, beta_outer, beta_reach = (blocks[2], blocks[3], blocks[4], blocks[5])
    leading = jnp.concatenate([-complex_dot(beta_reach, alpha_inward), beta_outer], 2)
    return leading + complex_dot(complex_dot(beta_reach, alpha_inner), solved)


def order_spans(side_pts, edge_pts, keeping):
    lower_ext = 2 * side_pts + (edge_pts if keeping else 0)
    starts = [
        (0, side_pts),
        (lower_ext, side_pts),
        (side_pts, side_pts),
        (lower_ext + side_pts, side_pts),
    ]
    if keeping:
        starts = starts + [(2 * side_pts, edge_pts), (lower_ext + 2 * side_pts, edge_pts)]
    return [(start_at, start_at + length) for start_at, length in starts]


def merge_boxes(map_lower, map_upper, side_pts, edge_pts, keeping):
    blocks, solved = merge_setup(map_lower, map_upper, side_pts, edge_pts, keeping)
    merged = jnp.concatenate([rows_lower(blocks, solved), rows_upper(blocks, solved)], 1)
    span_list = order_spans(side_pts, edge_pts, keeping)
    return block_take(merged, span_list, span_list)


def incident(position, thetas, face_pts, edge_pts):
    heights = (jnp.arange(face_pts, dtype=jnp.float32) + 0.5) / edge_pts
    across_x = jnp.cos(thetas)[:, None]
    along_y = jnp.sin(thetas)[:, None]
    left_phase = wavenumber * (position * across_x + heights[None, :] * along_y)
    right_phase = wavenumber * ((position + 1.0) * across_x + heights[None, :] * along_y)
    phases = jnp.concatenate([left_phase, right_phase], 1)
    return jnp.stack([jnp.cos(phases), jnp.sin(phases)])


def shifted_along(x, axis, pairs):
    return lax.ppermute(x, axis, pairs)


def role_spans(side_pts, edge_pts, keeping, lower):
    total_pts = 2 * side_pts + 2 * edge_pts
    if lower:
        outer = [(0, 2 * side_pts + (edge_pts if keeping else 0))]
        inner = [(2 * side_pts + edge_pts, total_pts)]
    else:
        outer = [(0, 2 * side_pts)] + ([(2 * side_pts + edge_pts, total_pts)] if keeping else [])
        inner = [(2 * side_pts, 2 * side_pts + edge_pts)]
    return outer, inner


def split_map(matrix, side_pts, edge_pts, keeping, lower):
    outer, inner = role_spans(side_pts, edge_pts, keeping, lower)
    cols = outer + inner
    return block_take(matrix, inner, cols), block_take(matrix, outer, cols)


def merge_parts(lower_in, lower_out, upper_in, upper_out, side_pts, edge_pts, keeping):
    n_ao = lower_out.shape[1]
    n_bo = upper_out.shape[1]
    alpha_outer = lower_out[:, :, :n_ao]
    alpha_reach = lower_out[:, :, n_ao:]
    alpha_inward = lower_in[:, :, :n_ao]
    alpha_inner = lower_in[:, :, n_ao:]
    beta_outer = upper_out[:, :, :n_bo]
    beta_reach = upper_out[:, :, n_bo:]
    beta_inward = upper_in[:, :, :n_bo]
    beta_inner = upper_in[:, :, n_bo:]
    identity_mat = jnp.stack(
        [jnp.eye(edge_pts, dtype=jnp.float32), jnp.zeros((edge_pts, edge_pts), jnp.float32)]
    )
    system = identity_mat - complex_dot(beta_inner, alpha_inner)
    right_mat = jnp.concatenate([-complex_dot(beta_inner, alpha_inward), beta_inward], 2)
    solved = complex_solve(system, right_mat)
    blocks = (alpha_outer, alpha_reach, alpha_inward, alpha_inner, beta_outer, beta_reach)
    merged = jnp.concatenate([rows_lower(blocks, solved), rows_upper(blocks, solved)], 1)
    span_list = order_spans(side_pts, edge_pts, keeping)
    return block_take(merged, span_list, span_list)


def exchange_merge(own, spare, own_is_lower, axis, apart, side_pts, edge_pts, keeping):
    spare_lo = split_map(spare, side_pts, edge_pts, keeping, True)
    spare_up = split_map(spare, side_pts, edge_pts, keeping, False)
    send_in = jnp.where(own_is_lower, spare_lo[0], spare_up[0])
    send_out = jnp.where(own_is_lower, spare_lo[1], spare_up[1])
    got_in = from_partner(send_in, axis, apart)
    got_in, send_out = lax.optimization_barrier((got_in, send_out))
    got_out = from_partner(send_out, axis, apart)
    own_lo = split_map(own, side_pts, edge_pts, keeping, True)
    own_up = split_map(own, side_pts, edge_pts, keeping, False)
    lower_in = jnp.where(own_is_lower, own_lo[0], got_in)
    lower_out = jnp.where(own_is_lower, own_lo[1], got_out)
    upper_in = jnp.where(own_is_lower, got_in, own_up[0])
    upper_out = jnp.where(own_is_lower, got_out, own_up[1])
    return merge_parts(lower_in, lower_out, upper_in, upper_out, side_pts, edge_pts, keeping)


def real_block(matrix):
    return jnp.concatenate(
        [
            jnp.concatenate([matrix[0].T, matrix[1].T], 1),
            jnp.concatenate([-matrix[1].T, matrix[0].T], 1),
        ],
        0,
    )


def per_device(leaf_maps, angles):
    edge_pts = leaf_maps.shape[-1] // 4
    leaf_id = lax.axis_index("leaf")
    pol_id = leaf_id % 2
    half_id = leaf_id // 2
    own_maps = leaf_maps[0, 0]
    own_pol = lax.dynamic_index_in_dim(own_maps, pol_id, 0, keepdims=False)
    other_pol = lax.dynamic_index_in_dim(own_maps, 1 - pol_id, 0, keepdims=False)
    paired = exchange_merge(own_pol, other_pol, pol_id == 0, "leaf", 0, edge_pts, edge_pts, True)
    full_map = exchange_merge(paired, paired, half_id == 0, "leaf", 1, 2 * edge_pts, edge_pts, False)
    face_pts = full_map.shape[1] // 2
    col_count = angles.shape[0] // 2
    thetas = lax.dynamic_slice_in_dim(angles, half_id * col_count, col_count)
    wide_id = lax.axis_index("wide")
    wide_count = lax.axis_size("wide")
    position = wide_id.astype(jnp.float32)
    incoming = incident(position, thetas, face_pts, edge_pts)
    driven = complex_apply(full_map, incoming)
    transfer = full_map[:, face_pts:, :face_pts]
    outgoing = driven[:, :, face_pts:]

    to_odd = [(i, i + 1) for i in range(0, wide_count, 2)]
    handed = shifted_along(jnp.concatenate([transfer, outgoing], 1), "wide", to_odd)
    prev_transfer = handed[:, :face_pts]
    prev_outgoing = handed[:, face_pts:]
    double_map = complex_dot(transfer, prev_transfer)
    double_drive = outgoing + complex_apply(transfer, prev_outgoing)
    to_quad = [(i, i + 2) for i in range(1, wide_count, 4)]
    handed2 = shifted_along(jnp.concatenate([double_map, double_drive], 1), "wide", to_quad)
    prev_double_map = handed2[:, :face_pts]
    prev_double_drive = handed2[:, face_pts:]
    quad_map = real_block(complex_dot(double_map, prev_double_map))
    quad_drive = double_drive + complex_apply(double_map, prev_double_drive)
    flat_drive = jnp.concatenate([quad_drive[0], quad_drive[1]], 1)
    blank = jnp.zeros_like(flat_drive)

    quad_pairs = [(i, i + 4) for i in range(3, wide_count - 4, 4)]

    def advance(step_at, stored):
        active = wide_id == 4 * step_at + 3
        sending = lax.cond(
            active,
            lambda: flat_drive
            + jnp.dot(stored, quad_map, precision=lax.Precision.HIGH, preferred_element_type=jnp.float32),
            lambda: blank,
        )
        received = shifted_along(sending, "wide", quad_pairs)
        return jnp.where(wide_id == 4 * step_at + 7, received, stored)

    flat_in = lax.fori_loop(0, wide_count // 4 - 1, advance, blank)
    quad_in = jnp.stack([flat_in[:, :face_pts], flat_in[:, face_pts:]])
    back_pairs = [(i + 2, i) for i in range(1, wide_count, 4)]
    given2 = shifted_along(quad_in, "wide", back_pairs)
    own_next = prev_double_drive + complex_apply(prev_double_map, quad_in)
    even_in = jnp.where(wide_id % 4 == 3, own_next, given2)
    to_even = [(i + 1, i) for i in range(0, wide_count, 2)]
    given = shifted_along(even_in, "wide", to_even)
    is_odd = wide_id % 2 == 1
    odd_in = prev_outgoing + complex_apply(prev_transfer, even_in)
    chained = jnp.where(is_odd, odd_in, given)
    right_part = outgoing + complex_apply(transfer, chained)
    left_part = driven[:, :, :face_pts] + complex_apply(full_map[:, :face_pts, :face_pts], chained)
    return (left_part[None], right_part[None])


def solution(mesh):
    placed = (P("wide", "leaf", None, None, None, None), P())
    return jax.shard_map(
        per_device,
        mesh=mesh,
        in_specs=placed,
        out_specs=(P("wide", None, "leaf", None), P("wide", None, "leaf", None)),
        check_vma=False,
    )
```

profile of v0, /device:TPU:59, one launch (start us, length us, event | category | flops | bytes accessed | tf_op | source)
XLA Modules:
  0.0 564.0 jit_solution(12720960103317303368)
XLA Ops:
  0.7 2.9 dynamic-slice_bitcast_fusion.1
  10.0 3.1 fusion.8
  13.2 6.1 %collective-permute-done.1 = f32[2,128,512]{2,1,0:T(8,128)} collective-permute-done((f32[2,128,512]{2,1,0:T(8,128)}, f32[2,128,512]{2,1,0:T(8,128)}, u32[]{:S(2)}, u32[]{:S(2)}) %collective-permute-start.1) | collective-permute-done | bytes 524320 | tf_op jit(solution)/shard_map/ppermute | solution.py:11
  25.2 11.7 %cholesky.130 = f32[128,128]{1,0:T(8,128)S(1)} custom-call(f32[128,128]{1,0:T(8,128)S(1)} %cholesky.194), custom_call_target="Cholesky" | custom-call | tf_op jit(solution)/shard_map/jit(cholesky)/cholesky | solution.py:66
  36.9 9.8 %custom-call.26 = f32[1,128,128]{1,2,0:T(8,128)S(1)} custom-call(f32[1,128,128]{2,1,0:T(8,128)S(1)} %get-tuple-element.251), custom_call_target="InvertDiagBlocksLowerTriangular" | custom-call | tf_op jit(solution)/shard_map/jit(cholesky)/cholesky | solution.py:66
  47.3 11.9 %cholesky.147 = f32[128,128]{1,0:T(8,128)S(1)} custom-call(f32[128,128]{1,0:T(8,128)S(1)} %convolution_subtract_fusion.16), custom_call_target="Cholesky" | custom-call | tf_op jit(solution)/shard_map/jit(cholesky)/cholesky | solution.py:66
  61.3 3.8 while.16
  65.1 19.7 %custom-call.22 = f32[2,128,128]{1,2,0:T(8,128)S(1)} custom-call(f32[2,128,128]{2,1,0:T(8,128)S(1)} %get-tuple-element.129), custom_call_target="InvertDiagBlocksLowerTriangular" | custom-call | tf_op jit(solution)/shard_map/jit(_cho_solve)/triangular_solve | solution.py:67
  93.0 26.5 %collective-permute-done.2 = f32[2,384,512]{2,1,0:T(8,128)S(1)} collective-permute-done((f32[2,384,512]{2,1,0:T(8,128)}, f32[2,384,512]{2,1,0:T(8,128)S(1)}, u32[]{:S(2)}, u32[]{:S(2)}) %collective-permute-start.2) | collective-permute-done | bytes 1572896 | tf_op jit(solution)/shard_map/ppermute | solution.py:11
  128.7 13.6 %fusion.91 = f32[384,768]{1,0:T(8,128)S(1)} fusion(f32[128,768]{1,0:T(8,128)S(1)} %fusion.111, f32[2,384,512]{2,1,0:T(8,128)S(1)} %get-tuple-element.228), kind=kOutput, calls=%fused_computation.236 | convolution fusion | flops 452984832 | bytes 1769472 | tf_op jit(solution)/shard_map/dot_general | solution.py:21
  151.3 11.5 %collective-permute-done.3 = f32[2,128,640]{2,1,0:T(8,128)S(1)} collective-permute-done((f32[2,128,640]{2,1,0:T(8,128)S(1)}, f32[2,128,640]{2,1,0:T(8,128)S(1)}, u32[]{:S(2)}, u32[]{:S(2)}) %collective-permute-start.3) | collective-permute-done | bytes 655392 | tf_op jit(solution)/shard_map/ppermute | solution.py:11
  166.6 11.7 %cholesky.164 = f32[128,128]{1,0:T(8,128)S(1)} custom-call(f32[128,128]{1,0:T(8,128)S(1)} %cholesky.197), custom_call_target="Cholesky" | custom-call | tf_op jit(solution)/shard_map/jit(cholesky)/cholesky | solution.py:66
  178.9 9.8 %custom-call.27 = f32[1,128,128]{1,2,0:T(8,128)S(1)} custom-call(f32[1,128,128]{2,1,0:T(8,128)S(1)} %get-tuple-element.247), custom_call_target="InvertDiagBlocksLowerTriangular" | custom-call | tf_op jit(solution)/shard_map/jit(cholesky)/cholesky | solution.py:66
  190.9 11.7 %cholesky.181 = f32[128,128]{1,0:T(8,128)S(1)} custom-call(f32[128,128]{1,0:T(8,128)S(1)} %convolution_subtract_fusion.14), custom_call_target="Cholesky" | custom-call | tf_op jit(solution)/shard_map/jit(cholesky)/cholesky | solution.py:66
  204.6 3.8 while.17
  208.4 20.7 %custom-call.23 = f32[2,128,128]{1,2,0:T(8,128)} custom-call(f32[2,128,128]{2,1,0:T(8,128)S(1)} %get-tuple-element.137), custom_call_target="InvertDiagBlocksLowerTriangular" | custom-call | tf_op jit(solution)/shard_map/jit(_cho_solve)/triangular_solve | solution.py:67
  241.9 44.1 %collective-permute-done.4 = f32[2,512,640]{2,1,0:T(8,128)S(1)} collective-permute-done((f32[2,512,640]{2,1,0:T(8,128)}, f32[2,512,640]{2,1,0:T(8,128)S(1)}, u32[]{:S(2)}, u32[]{:S(2)}) %collective-permute-start.4) | collective-permute-done | bytes 2621472 | tf_op jit(solution)/shard_map/ppermute | solution.py:11
  314.3 3.7 fusion
  318.0 3.7 fusion.1
  321.7 3.7 fusion.24
  325.4 3.9 fusion.22
  332.1 6.5 %collective-permute-done.5 = f32[2,528,512]{2,1,0:T(8,128)S(1)} collective-permute-done((f32[2,528,512]{2,1,0:T(8,128)S(1)}, f32[2,528,512]{2,1,0:T(8,128)S(1)}, u32[]{:S(2)}, u32[]{:S(2)}) %collective-permute-start.5) | collective-permute-done | bytes 2162720 | tf_op jit(solution)/shard_map/ppermute | solution.py:147
  353.3 26.2 %collective-permute-done.6 = f32[2,528,512]{2,1,0:T(8,128)} collective-permute-done((f32[2,528,512]{2,1,0:T(8,128)}, f32[2,528,512]{2,1,0:T(8,128)}, u32[]{:S(2)}, u32[]{:S(2)}) %collective-permute-start.6) | collective-permute-done | bytes 2162720 | tf_op jit(solution)/shard_map/ppermute | solution.py:147
  387.5 3.1 fusion.57
  390.6 3.1 fusion.59
  393.7 3.2 convolution_subtract_fusion.2
  396.9 3.2 fusion.170
  402.5 5.6 copy.14
  408.1 129.9 %while.18 = (s32[]{:T(128)}, f32[16,1024]{1,0:T(8,128)S(1)}, s32[]{:T(128)}, f32[1024,1024]{1,0:T(8,128)}, f32[16,1024]{1,0:T(8,128)S(1)}, /*index=5*/s32[]{:T(128)}, s32[]{:T(128)}, s32[]{:T(128)}, s32[]{:T(128)}, s32[]{:T(128)}) while((s32[]{:T(128)}, f32[16,1024]{1,0:T(8,128)S(1)}, s32[]{:T(128)}, f32[1024,1024]{1,0:T(8,128)}, ...), condition=%wide.region_7.9_spmd.clone, body=%wide.region_4.8_spmd.clone.sunk | while | flops 100728840 | bytes 4980980 | solution.py:266
  408.1 4.9 collective-permute-start
  413.0 3.9 collective-permute-done
  419.6 5.4 collective-permute-done
  427.1 6.1 %collective-permute-done = f32[16,1024]{1,0:T(8,128)S(1)} collective-permute-done((f32[16,1024]{1,0:T(8,128)S(1)}, f32[16,1024]{1,0:T(8,128)S(1)}, u32[]{:S(2)}, u32[]{:S(2)}) %collective-permute-start) | collective-permute-done | bytes 65568 | tf_op jit(solution)/shard_map/while/body/eval_jaxpr/ppermute | solution.py:147
  435.2 6.1 %collective-permute-done = f32[16,1024]{1,0:T(8,128)S(1)} collective-permute-done((f32[16,1024]{1,0:T(8,128)S(1)}, f32[16,1024]{1,0:T(8,128)S(1)}, u32[]{:S(2)}, u32[]{:S(2)}) %collective-permute-start) | collective-permute-done | bytes 65568 | tf_op jit(solution)/shard_map/while/body/eval_jaxpr/ppermute | solution.py:147
  443.4 6.1 %collective-permute-done = f32[16,1024]{1,0:T(8,128)S(1)} collective-permute-done((f32[16,1024]{1,0:T(8,128)S(1)}, f32[16,1024]{1,0:T(8,128)S(1)}, u32[]{:S(2)}, u32[]{:S(2)}) %collective-permute-start) | collective-permute-done | bytes 65568 | tf_op jit(solution)/shard_map/while/body/eval_jaxpr/ppermute | solution.py:147
  451.5 6.1 %collective-permute-done = f32[16,1024]{1,0:T(8,128)S(1)} collective-permute-done((f32[16,1024]{1,0:T(8,128)S(1)}, f32[16,1024]{1,0:T(8,128)S(1)}, u32[]{:S(2)}, u32[]{:S(2)}) %collective-permute-start) | collective-permute-done | bytes 65568 | tf_op jit(solution)/shard_map/while/body/eval_jaxpr/ppermute | solution.py:147
  459.6 6.1 %collective-permute-done = f32[16,1024]{1,0:T(8,128)S(1)} collective-permute-done((f32[16,1024]{1,0:T(8,128)S(1)}, f32[16,1024]{1,0:T(8,128)S(1)}, u32[]{:S(2)}, u32[]{:S(2)}) %collective-permute-start) | collective-permute-done | bytes 65568 | tf_op jit(solution)/shard_map/while/body/eval_jaxpr/ppermute | solution.py:147
  467.7 6.1 %collective-permute-done = f32[16,1024]{1,0:T(8,128)S(1)} collective-permute-done((f32[16,1024]{1,0:T(8,128)S(1)}, f32[16,1024]{1,0:T(8,128)S(1)}, u32[]{:S(2)}, u32[]{:S(2)}) %collective-permute-start) | collective-permute-done | bytes 65568 | tf_op jit(solution)/shard_map/while/body/eval_jaxpr/ppermute | solution.py:147
  475.8 6.1 %collective-permute-done = f32[16,1024]{1,0:T(8,128)S(1)} collective-permute-done((f32[16,1024]{1,0:T(8,128)S(1)}, f32[16,1024]{1,0:T(8,128)S(1)}, u32[]{:S(2)}, u32[]{:S(2)}) %collective-permute-start) | collective-permute-done | bytes 65568 | tf_op jit(solution)/shard_map/while/body/eval_jaxpr/ppermute | solution.py:147
  483.9 6.1 %collective-permute-done = f32[16,1024]{1,0:T(8,128)S(1)} collective-permute-done((f32[16,1024]{1,0:T(8,128)S(1)}, f32[16,1024]{1,0:T(8,128)S(1)}, u32[]{:S(2)}, u32[]{:S(2)}) %collective-permute-start) | collective-permute-done | bytes 65568 | tf_op jit(solution)/shard_map/while/body/eval_jaxpr/ppermute | solution.py:147
  492.1 6.1 %collective-permute-done = f32[16,1024]{1,0:T(8,128)S(1)} collective-permute-done((f32[16,1024]{1,0:T(8,128)S(1)}, f32[16,1024]{1,0:T(8,128)S(1)}, u32[]{:S(2)}, u32[]{:S(2)}) %collective-permute-start) | collective-permute-done | bytes 65568 | tf_op jit(solution)/shard_map/while/body/eval_jaxpr/ppermute | solution.py:147
  500.2 10.1 %collective-permute-done = f32[16,1024]{1,0:T(8,128)S(1)} collective-permute-done((f32[16,1024]{1,0:T(8,128)S(1)}, f32[16,1024]{1,0:T(8,128)S(1)}, u32[]{:S(2)}, u32[]{:S(2)}) %collective-permute-start) | collective-permute-done | bytes 65568 | tf_op jit(solution)/shard_map/while/body/eval_jaxpr/ppermute | solution.py:147
  510.3 3.4 conditional.3
  510.3 3.3 convolution_add_fusion
  515.6 6.1 %collective-permute-done = f32[16,1024]{1,0:T(8,128)S(1)} collective-permute-done((f32[16,1024]{1,0:T(8,128)S(1)}, f32[16,1024]{1,0:T(8,128)S(1)}, u32[]{:S(2)}, u32[]{:S(2)}) %collective-permute-start) | collective-permute-done | bytes 65568 | tf_op jit(solution)/shard_map/while/body/eval_jaxpr/ppermute | solution.py:147
  521.8 3.1 collective-permute-start
  524.9 4.9 collective-permute-done
  531.8 6.1 %collective-permute-done = f32[16,1024]{1,0:T(8,128)S(1)} collective-permute-done((f32[16,1024]{1,0:T(8,128)S(1)}, f32[16,1024]{1,0:T(8,128)S(1)}, u32[]{:S(2)}, u32[]{:S(2)}) %collective-permute-start) | collective-permute-done | bytes 65568 | tf_op jit(solution)/shard_map/while/body/eval_jaxpr/ppermute | solution.py:147
  (382 shorter events, 174.5 us)
Async XLA Ops:
  3.5 4.2 copy-start.12
  6.1 13.1 %collective-permute-start.1 = (f32[2,128,512]{2,1,0:T(8,128)}, f32[2,128,512]{2,1,0:T(8,128)}, u32[]{:S(2)}, u32[]{:S(2)}) collective-permute-start(f32[2,128,512]{2,1,0:T(8,128)} %get-tuple-element.224), channel_id=1, source_target_pairs={{0,1},{1,0},{2,3},{3,2},{4,5},{5,4},{6,7},{7,6},{8,9},{9,8},{10,11... | collective-permute-start | bytes 1572872 | tf_op jit(solution)/shard_map/ppermute | solution.py:11
  10.0 9.2 %copy-start.36 = (f32[2,128,128]{2,1,0:T(8,128)S(1)}, f32[2,128,128]{2,1,0:T(8,128)}, u32[]{:S(2)}) copy-start(f32[2,128,128]{2,1,0:T(8,128)} %get-tuple-element.221) | copy-start | bytes 393220
  10.0 9.2 %copy-start.37 = (f32[2,128,128]{2,1,0:T(8,128)S(1)}, f32[2,128,128]{2,1,0:T(8,128)}, u32[]{:S(2)}) copy-start(f32[2,128,128]{2,1,0:T(8,128)} %get-tuple-element.222) | copy-start | bytes 393220
  20.6 3.9 copy-start.16
  20.7 67.4 %copy-start.21 = (f32[2,128,512]{2,1,0:T(8,128)}, f32[2,128,512]{2,1,0:T(8,128)S(1)}, u32[]{:S(2)}) copy-start(f32[2,128,512]{2,1,0:T(8,128)S(1)} %get-tuple-element.219) | copy-start | bytes 1572868
  24.6 36.6 %copy-start.46 = (s32[2]{0:T(128)S(1)}, s32[2]{0:T(128)}, u32[]{:S(2)}) copy-start(s32[2]{0:T(128)} %iota_multiply_fusion) | copy-start | bytes 28
  65.1 23.0 %copy-start.44 = (s32[2,2]{1,0:T(2,128)}, s32[2,2]{1,0:T(2,128)S(1)}, u32[]{:S(2)}) copy-start(s32[2,2]{1,0:T(2,128)S(1)} %get-tuple-element.431) | copy-start | bytes 52
  84.8 34.7 %collective-permute-start.2 = (f32[2,384,512]{2,1,0:T(8,128)}, f32[2,384,512]{2,1,0:T(8,128)S(1)}, u32[]{:S(2)}, u32[]{:S(2)}) collective-permute-start(f32[2,384,512]{2,1,0:T(8,128)} %fusion.8), channel_id=1, source_target_pairs={{0,1},{1,0},{2,3},{3,2},{4,5},{5,4},{6,7},{7,6},{8,9},{9,8},{10,11... | collective-permute-start | bytes 4718600 | tf_op jit(solution)/shard_map/ppermute | solution.py:11
  89.1 30.3 %copy-start.13 = (f32[2,512,512]{2,1,0:T(8,128)S(1)}, f32[2,512,512]{2,1,0:T(8,128)}, u32[]{:S(2)}) copy-start(f32[2,512,512]{2,1,0:T(8,128)} %copy-done.12) | copy-start | bytes 6291460
  89.2 30.3 %copy-start.22 = (f32[2,128,512]{2,1,0:T(8,128)S(1)}, f32[2,128,512]{2,1,0:T(8,128)}, u32[]{:S(2)}) copy-start(f32[2,128,512]{2,1,0:T(8,128)} %copy-done.21) | copy-start | bytes 1572868
  93.0 27.0 %copy-start.17 = (f32[2,128,512]{2,1,0:T(8,128)S(1)}, f32[2,128,512]{2,1,0:T(8,128)}, u32[]{:S(2)}) copy-start(f32[2,128,512]{2,1,0:T(8,128)} %copy-done.16) | copy-start | bytes 1572868
  147.4 15.5 %collective-permute-start.3 = (f32[2,128,640]{2,1,0:T(8,128)S(1)}, f32[2,128,640]{2,1,0:T(8,128)S(1)}, u32[]{:S(2)}, u32[]{:S(2)}) collective-permute-start(f32[2,128,640]{2,1,0:T(8,128)S(1)} %get-tuple-element.187), channel_id=1, source_target_pairs={{0,2},{1,3},{2,0},{3,1},{4,6},{5,7},{6,4},{7,5},{8,10},{9,11},{10,... | collective-permute-start | bytes 1966088 | tf_op jit(solution)/shard_map/ppermute | solution.py:11
  163.0 71.6 %copy-start.10 = (f32[2,128,640]{2,1,0:T(8,128)}, f32[2,128,640]{2,1,0:T(8,128)S(1)}, u32[]{:S(2)}) copy-start(f32[2,128,640]{2,1,0:T(8,128)S(1)} %get-tuple-element.234) | copy-start | bytes 1966084
  164.3 40.2 %copy-start.41 = (f32[128,128]{0,1:T(8,128)}, f32[128,128]{0,1:T(8,128)S(1)}, u32[]{:S(2)}) copy-start(f32[128,128]{0,1:T(8,128)S(1)} %get-tuple-element.237) | copy-start | bytes 196612
  164.3 40.3 %copy-start.45 = (s32[2,2]{1,0:T(2,128)S(1)}, s32[2,2]{1,0:T(2,128)}, u32[]{:S(2)}) copy-start(s32[2,2]{1,0:T(2,128)} %copy-done.44) | copy-start | bytes 52
  229.1 56.9 %collective-permute-start.4 = (f32[2,512,640]{2,1,0:T(8,128)}, f32[2,512,640]{2,1,0:T(8,128)S(1)}, u32[]{:S(2)}, u32[]{:S(2)}) collective-permute-start(f32[2,512,640]{2,1,0:T(8,128)} %broadcast_select_fusion.4), channel_id=1, source_target_pairs={{0,2},{1,3},{2,0},{3,1},{4,6},{5,7},{6,4},{7,5},{8,10},{9,11},{10,... | collective-permute-start | bytes 7864328 | tf_op jit(solution)/shard_map/ppermute | solution.py:11
  240.0 46.0 %copy-start.24 = (f32[2,128,768]{2,1,0:T(8,128)S(1)}, f32[2,128,768]{2,1,0:T(8,128)}, u32[]{:S(2)}) copy-start(f32[2,128,768]{2,1,0:T(8,128)} %copy-done.23) | copy-start | bytes 2359300
  240.0 46.0 %copy-start.26 = (f32[2,128,768]{2,1,0:T(8,128)S(1)}, f32[2,128,768]{2,1,0:T(8,128)}, u32[]{:S(2)}) copy-start(f32[2,128,768]{2,1,0:T(8,128)} %copy-done.25) | copy-start | bytes 2359300
  240.0 46.0 %copy-start.28 = (f32[2,128,768]{2,1,0:T(8,128)S(1)}, f32[2,128,768]{2,1,0:T(8,128)}, u32[]{:S(2)}) copy-start(f32[2,128,768]{2,1,0:T(8,128)} %copy-done.27) | copy-start | bytes 2359300
  240.0 46.0 %copy-start.30 = (f32[2,128,768]{2,1,0:T(8,128)S(1)}, f32[2,128,768]{2,1,0:T(8,128)}, u32[]{:S(2)}) copy-start(f32[2,128,768]{2,1,0:T(8,128)} %copy-done.29) | copy-start | bytes 2359300
  241.9 44.9 %copy-start.11 = (f32[2,128,640]{2,1,0:T(8,128)S(1)}, f32[2,128,640]{2,1,0:T(8,128)}, u32[]{:S(2)}) copy-start(f32[2,128,640]{2,1,0:T(8,128)} %copy-done.10) | copy-start | bytes 1966084
  312.3 18.5 %copy-start = (f32[2,1024,256]{2,1,0:T(8,128)}, f32[2,1024,256]{2,1,0:T(8,128)S(1)}, u32[]{:S(2)}) copy-start(f32[2,1024,256]{2,1,0:T(8,128)S(1)} %get-tuple-element.196) | copy-start | bytes 6291460
  329.5 9.1 %collective-permute-start.5 = (f32[2,528,512]{2,1,0:T(8,128)S(1)}, f32[2,528,512]{2,1,0:T(8,128)S(1)}, u32[]{:S(2)}, u32[]{:S(2)}) collective-permute-start(f32[2,528,512]{2,1,0:T(8,128)S(1)} %pad_maximum_fusion.5), channel_id=1, source_target_pairs={{0,4},{8,12},{16,20},{24,28},{32,36},{40,44},{48,52},{56,60},{64,6... | collective-permute-start | bytes 6488072 | tf_op jit(solution)/shard_map/ppermute | solution.py:147
  332.1 16.1 %copy-start.2 = (f32[512,512]{1,0:T(8,128)}, f32[512,512]{1,0:T(8,128)S(1)}, u32[]{:S(2)}) copy-start(f32[512,512]{1,0:T(8,128)S(1)} %get-tuple-element.205) | copy-start | bytes 3145732
  338.7 9.5 %copy-start.8 = (f32[2,528,512]{2,1,0:T(8,128)}, f32[2,528,512]{2,1,0:T(8,128)S(1)}, u32[]{:S(2)}) copy-start(f32[2,528,512]{2,1,0:T(8,128)S(1)} %collective-permute-done.5) | copy-start | bytes 6488068
  351.8 27.8 %collective-permute-start.6 = (f32[2,528,512]{2,1,0:T(8,128)}, f32[2,528,512]{2,1,0:T(8,128)}, u32[]{:S(2)}, u32[]{:S(2)}) collective-permute-start(f32[2,528,512]{2,1,0:T(8,128)} %pad_maximum_fusion.6), channel_id=1, source_target_pairs={{4,12},{20,28},{36,44},{52,60},{68,76},{84,92},{100,108},{116,124}... | collective-permute-start | bytes 6488072 | tf_op jit(solution)/shard_map/ppermute | solution.py:147
  353.3 30.7 %copy-start.5 = (f32[512,512]{1,0:T(8,128)S(1)}, f32[512,512]{1,0:T(8,128)}, u32[]{:S(2)}) copy-start(f32[512,512]{1,0:T(8,128)} %copy-done.4) | copy-start | bytes 3145732
  353.3 32.4 %copy-start.7 = (f32[512,512]{1,0:T(8,128)S(1)}, f32[512,512]{1,0:T(8,128)}, u32[]{:S(2)}) copy-start(f32[512,512]{1,0:T(8,128)} %copy-done.6) | copy-start | bytes 3145732
  408.1 8.9 %collective-permute-start = (f32[16,1024]{1,0:T(8,128)S(1)}, f32[16,1024]{1,0:T(8,128)S(1)}, u32[]{:S(2)}, u32[]{:S(2)}) collective-permute-start(f32[16,1024]{1,0:T(8,128)S(1)} %get-tuple-element.414), channel_id=1, source_target_pairs={{12,28},{28,44},{44,60},{60,76},{76,92},{92,108},{108,124},{124,14... | collective-permute-start | bytes 196616 | tf_op jit(solution)/shard_map/while/body/eval_jaxpr/ppermute | solution.py:147
  417.1 8.0 %collective-permute-start = (f32[16,1024]{1,0:T(8,128)S(1)}, f32[16,1024]{1,0:T(8,128)S(1)}, u32[]{:S(2)}, u32[]{:S(2)}) collective-permute-start(f32[16,1024]{1,0:T(8,128)S(1)} %get-tuple-element.414), channel_id=1, source_target_pairs={{12,28},{28,44},{44,60},{60,76},{76,92},{92,108},{108,124},{124,14... | collective-permute-start | bytes 196616 | tf_op jit(solution)/shard_map/while/body/eval_jaxpr/ppermute | solution.py:147
  425.2 8.0 %collective-permute-start = (f32[16,1024]{1,0:T(8,128)S(1)}, f32[16,1024]{1,0:T(8,128)S(1)}, u32[]{:S(2)}, u32[]{:S(2)}) collective-permute-start(f32[16,1024]{1,0:T(8,128)S(1)} %get-tuple-element.414), channel_id=1, source_target_pairs={{12,28},{28,44},{44,60},{60,76},{76,92},{92,108},{108,124},{124,14... | collective-permute-start | bytes 196616 | tf_op jit(solution)/shard_map/while/body/eval_jaxpr/ppermute | solution.py:147
  433.3 8.0 %collective-permute-start = (f32[16,1024]{1,0:T(8,128)S(1)}, f32[16,1024]{1,0:T(8,128)S(1)}, u32[]{:S(2)}, u32[]{:S(2)}) collective-permute-start(f32[16,1024]{1,0:T(8,128)S(1)} %get-tuple-element.414), channel_id=1, source_target_pairs={{12,28},{28,44},{44,60},{60,76},{76,92},{92,108},{108,124},{124,14... | collective-permute-start | bytes 196616 | tf_op jit(solution)/shard_map/while/body/eval_jaxpr/ppermute | solution.py:147
  441.4 8.0 %collective-permute-start = (f32[16,1024]{1,0:T(8,128)S(1)}, f32[16,1024]{1,0:T(8,128)S(1)}, u32[]{:S(2)}, u32[]{:S(2)}) collective-permute-start(f32[16,1024]{1,0:T(8,128)S(1)} %get-tuple-element.414), channel_id=1, source_target_pairs={{12,28},{28,44},{44,60},{60,76},{76,92},{92,108},{108,124},{124,14... | collective-permute-start | bytes 196616 | tf_op jit(solution)/shard_map/while/body/eval_jaxpr/ppermute | solution.py:147
  449.5 8.0 %collective-permute-start = (f32[16,1024]{1,0:T(8,128)S(1)}, f32[16,1024]{1,0:T(8,128)S(1)}, u32[]{:S(2)}, u32[]{:S(2)}) collective-permute-start(f32[16,1024]{1,0:T(8,128)S(1)} %get-tuple-element.414), channel_id=1, source_target_pairs={{12,28},{28,44},{44,60},{60,76},{76,92},{92,108},{108,124},{124,14... | collective-permute-start | bytes 196616 | tf_op jit(solution)/shard_map/while/body/eval_jaxpr/ppermute | solution.py:147
  457.6 8.0 %collective-permute-start = (f32[16,1024]{1,0:T(8,128)S(1)}, f32[16,1024]{1,0:T(8,128)S(1)}, u32[]{:S(2)}, u32[]{:S(2)}) collective-permute-start(f32[16,1024]{1,0:T(8,128)S(1)} %get-tuple-element.414), channel_id=1, source_target_pairs={{12,28},{28,44},{44,60},{60,76},{76,92},{92,108},{108,124},{124,14... | collective-permute-start | bytes 196616 | tf_op jit(solution)/shard_map/while/body/eval_jaxpr/ppermute | solution.py:147
  465.8 8.0 %collective-permute-start = (f32[16,1024]{1,0:T(8,128)S(1)}, f32[16,1024]{1,0:T(8,128)S(1)}, u32[]{:S(2)}, u32[]{:S(2)}) collective-permute-start(f32[16,1024]{1,0:T(8,128)S(1)} %get-tuple-element.414), channel_id=1, source_target_pairs={{12,28},{28,44},{44,60},{60,76},{76,92},{92,108},{108,124},{124,14... | collective-permute-start | bytes 196616 | tf_op jit(solution)/shard_map/while/body/eval_jaxpr/ppermute | solution.py:147
  473.9 8.0 %collective-permute-start = (f32[16,1024]{1,0:T(8,128)S(1)}, f32[16,1024]{1,0:T(8,128)S(1)}, u32[]{:S(2)}, u32[]{:S(2)}) collective-permute-start(f32[16,1024]{1,0:T(8,128)S(1)} %get-tuple-element.414), channel_id=1, source_target_pairs={{12,28},{28,44},{44,60},{60,76},{76,92},{92,108},{108,124},{124,14... | collective-permute-start | bytes 196616 | tf_op jit(solution)/shard_map/while/body/eval_jaxpr/ppermute | solution.py:147
  482.0 8.0 %collective-permute-start = (f32[16,1024]{1,0:T(8,128)S(1)}, f32[16,1024]{1,0:T(8,128)S(1)}, u32[]{:S(2)}, u32[]{:S(2)}) collective-permute-start(f32[16,1024]{1,0:T(8,128)S(1)} %get-tuple-element.414), channel_id=1, source_target_pairs={{12,28},{28,44},{44,60},{60,76},{76,92},{92,108},{108,124},{124,14... | collective-permute-start | bytes 196616 | tf_op jit(solution)/shard_map/while/body/eval_jaxpr/ppermute | solution.py:147
  490.1 8.0 %collective-permute-start = (f32[16,1024]{1,0:T(8,128)S(1)}, f32[16,1024]{1,0:T(8,128)S(1)}, u32[]{:S(2)}, u32[]{:S(2)}) collective-permute-start(f32[16,1024]{1,0:T(8,128)S(1)} %get-tuple-element.414), channel_id=1, source_target_pairs={{12,28},{28,44},{44,60},{60,76},{76,92},{92,108},{108,124},{124,14... | collective-permute-start | bytes 196616 | tf_op jit(solution)/shard_map/while/body/eval_jaxpr/ppermute | solution.py:147
  498.2 12.0 %collective-permute-start = (f32[16,1024]{1,0:T(8,128)S(1)}, f32[16,1024]{1,0:T(8,128)S(1)}, u32[]{:S(2)}, u32[]{:S(2)}) collective-permute-start(f32[16,1024]{1,0:T(8,128)S(1)} %get-tuple-element.414), channel_id=1, source_target_pairs={{12,28},{28,44},{44,60},{60,76},{76,92},{92,108},{108,124},{124,14... | collective-permute-start | bytes 196616 | tf_op jit(solution)/shard_map/while/body/eval_jaxpr/ppermute | solution.py:147
  513.7 8.0 %collective-permute-start = (f32[16,1024]{1,0:T(8,128)S(1)}, f32[16,1024]{1,0:T(8,128)S(1)}, u32[]{:S(2)}, u32[]{:S(2)}) collective-permute-start(f32[16,1024]{1,0:T(8,128)S(1)} %get-tuple-element.414), channel_id=1, source_target_pairs={{12,28},{28,44},{44,60},{60,76},{76,92},{92,108},{108,124},{124,14... | collective-permute-start | bytes 196616 | tf_op jit(solution)/shard_map/while/body/eval_jaxpr/ppermute | solution.py:147
  521.8 8.0 %collective-permute-start = (f32[16,1024]{1,0:T(8,128)S(1)}, f32[16,1024]{1,0:T(8,128)S(1)}, u32[]{:S(2)}, u32[]{:S(2)}) collective-permute-start(f32[16,1024]{1,0:T(8,128)S(1)} %get-tuple-element.414), channel_id=1, source_target_pairs={{12,28},{28,44},{44,60},{60,76},{76,92},{92,108},{108,124},{124,14... | collective-permute-start | bytes 196616 | tf_op jit(solution)/shard_map/while/body/eval_jaxpr/ppermute | solution.py:147
  529.9 8.0 %collective-permute-start = (f32[16,1024]{1,0:T(8,128)S(1)}, f32[16,1024]{1,0:T(8,128)S(1)}, u32[]{:S(2)}, u32[]{:S(2)}) collective-permute-start(f32[16,1024]{1,0:T(8,128)S(1)} %get-tuple-element.414), channel_id=1, source_target_pairs={{12,28},{28,44},{44,60},{60,76},{76,92},{92,108},{108,124},{124,14... | collective-permute-start | bytes 196616 | tf_op jit(solution)/shard_map/while/body/eval_jaxpr/ppermute | solution.py:147
  538.0 12.5 %copy-start.9 = (f32[2,528,512]{2,1,0:T(8,128)S(1)}, f32[2,528,512]{2,1,0:T(8,128)}, u32[]{:S(2)}) copy-start(f32[2,528,512]{2,1,0:T(8,128)} %copy-done.8) | copy-start | bytes 6488068
  538.0 10.2 %collective-permute-start.7 = (f32[2,16,512]{2,1,0:T(8,128)S(1)}, f32[2,16,512]{2,1,0:T(8,128)S(1)}, u32[]{:S(2)}, u32[]{:S(2)}) collective-permute-start(f32[2,16,512]{2,1,0:T(8,128)S(1)} %pad_maximum_fusion.16), channel_id=1, source_target_pairs={{12,4},{28,20},{44,36},{60,52},{76,68},{92,84},{108,100},{124,116}... | collective-permute-start | bytes 196616 | tf_op jit(solution)/shard_map/ppermute | solution.py:147
  549.0 5.4 copy-start.1
  549.0 5.4 collective-permute-start.8
  (22 other events, 51.8 us)
where the time goes:
time: 575 us; the launch traced here: 564 us
  waiting for transfers between devices  212 us (37%)
  matrix products  140 us (24%)
  other arithmetic  137 us (24%)
  starting transfers between devices  43.6 us (8%)
  local copies, waits for them, and re-layouts  25 us (4%)
    ppermute x19, waiting for transfers between devices, shifted_along(): return lax.ppermute(x, axis, pairs)  124 us
    ppermute x4, waiting for transfers between devices, from_partner(): lax.ppermute(x, axis, [(i, i ^ 1 << apart) for i in range(lax.axis_size(a...  88.2 us
    dot_general x56, matrix products, plain_dot(): jnp.dot(left_mat, right_mat, precision=precise, preferred_element_type=jn...  74.9 us
    another operation x13, other arithmetic, complex_solve(): factor = jnp.linalg.cholesky(normal)  68.8 us
    dot_general x28, matrix products, side_dot(): lax.dot_general(vectors, matrix, (((1,), (1,)), ((), ())), precision=prec...  47.2 us
    another operation x5, other arithmetic, complex_solve(): solution = jax.scipy.linalg.cho_solve((factor, True), projected)  41 us
    ppermute x19, starting transfers between devices, shifted_along(): return lax.ppermute(x, axis, pairs)  39.2 us
  transfers between devices with their start and end apart: 23, of which 21 were waited for; matrix products, arithmetic and copies ran while one was open for 7% of the time, Pallas kernels for 0%

commit v1 on v0

--- a/solution.py
+++ b/solution.py
@@ -9,12 +9,6 @@
 
 def from_partner(x, axis, apart):
     return lax.ppermute(x, axis, [(i, i ^ 1 << apart) for i in range(lax.axis_size(axis))])
-
-
-def passed_along(x, axis, by):
-    peers = lax.axis_size(axis)
-    pairs = [(i, i + by) for i in range(peers) if 0 <= i + by < peers]
-    return lax.ppermute(x, axis, pairs)
 
 
 def plain_dot(left_mat, right_mat):
@@ -73,31 +67,6 @@
     return jnp.concatenate([row_cat[:, :, start_at:stop_at] for start_at, stop_at in col_list], 2)
 
 
-def merge_setup(map_lower, map_upper, side_pts, edge_pts, keeping):
-    total_pts = 2 * side_pts + 2 * edge_pts
-    lower_ext = 2 * side_pts + (edge_pts if keeping else 0)
-    lower_outer = [(0, lower_ext)]
-    lower_inner = [(2 * side_pts + edge_pts, total_pts)]
-    upper_outer = [(0, 2 * side_pts)] + ([(2 * side_pts + edge_pts, total_pts)] if keeping else [])
-    upper_inner = [(2 * side_pts, 2 * side_pts + edge_pts)]
-    alpha_outer = block_take(map_lower, lower_outer, lower_outer)
-    alpha_reach = block_take(map_lower, lower_outer, lower_inner)
-    alpha_inward = block_take(map_lower, lower_inner, lower_outer)
-    alpha_inner = block_take(map_lower, lower_inner, lower_inner)
-    beta_outer = block_take(map_upper, upper_outer, upper_outer)
-    beta_reach = block_take(map_upper, upper_outer, upper_inner)
-    beta_inward = block_take(map_upper, upper_inner, upper_outer)
-    beta_inner = block_take(map_upper, upper_inner, upper_inner)
-    identity_mat = jnp.stack(
-        [jnp.eye(edge_pts, dtype=jnp.float32), jnp.zeros((edge_pts, edge_pts), jnp.float32)]
-    )
-    system = identity_mat - complex_dot(beta_inner, alpha_inner)
-    right_mat = jnp.concatenate([-complex_dot(beta_inner, alpha_inward), beta_inward], 2)
-    solved = complex_solve(system, right_mat)
-    blocks = (alpha_outer, alpha_reach, alpha_inward, alpha_inner, beta_outer, beta_reach)
-    return (blocks, solved)
-
-
 def rows_lower(blocks, solved):
     alpha_outer, alpha_reach = (blocks[0], blocks[1])
     upper_count = solved.shape[2] - alpha_outer.shape[2]
@@ -124,13 +93,6 @@
     if keeping:
         starts = starts + [(2 * side_pts, edge_pts), (lower_ext + 2 * side_pts, edge_pts)]
     return [(start_at, start_at + length) for start_at, length in starts]
-
-
-def merge_boxes(map_lower, map_upper, side_pts, edge_pts, keeping):
-    blocks, solved = merge_setup(map_lower, map_upper, side_pts, edge_pts, keeping)
-    merged = jnp.concatenate([rows_lower(blocks, solved), rows_upper(blocks, solved)], 1)
-    span_list = order_spans(side_pts, edge_pts, keeping)
-    return block_take(merged, span_list, span_list)
 
 
 def incident(position, thetas, face_pts, edge_pts):
@@ -214,7 +176,7 @@
     )
 
 
-def per_device(leaf_maps, angles):
+def per_device_body(leaf_maps, angles):
     edge_pts = leaf_maps.shape[-1] // 4
     leaf_id = lax.axis_index("leaf")
     pol_id = leaf_id % 2
@@ -282,7 +244,7 @@
 def solution(mesh):
     placed = (P("wide", "leaf", None, None, None, None), P())
     return jax.shard_map(
-        per_device,
+        per_device_body,
         mesh=mesh,
         in_specs=placed,
         out_specs=(P("wide", None, "leaf", None), P("wide", None, "leaf", None)),

time: 575 us -> 575 us (level)
  no operation moved by 1% of the time
where the time goes in v1:
time: 575 us; the launch traced here: 564 us
  waiting for transfers between devices  212 us (37%)
  matrix products  140 us (24%)
  other arithmetic  137 us (24%)
  starting transfers between devices  43.6 us (8%)
  local copies, waits for them, and re-layouts  25 us (4%)
    ppermute x19, waiting for transfers between devices, shifted_along(): return lax.ppermute(x, axis, pairs)  124 us
    ppermute x4, waiting for transfers between devices, from_partner(): lax.ppermute(x, axis, [(i, i ^ 1 << apart) for i in range(lax.axis_size(a...  88.2 us
    dot_general x56, matrix products, plain_dot(): jnp.dot(left_mat, right_mat, precision=precise, preferred_element_type=jn...  74.9 us
    another operation x13, other arithmetic, complex_solve(): factor = jnp.linalg.cholesky(normal)  68.8 us
    dot_general x28, matrix products, side_dot(): lax.dot_general(vectors, matrix, (((1,), (1,)), ((), ())), precision=prec...  47.2 us
    another operation x5, other arithmetic, complex_solve(): solution = jax.scipy.linalg.cho_solve((factor, True), projected)  41 us
    ppermute x19, starting transfers between devices, shifted_along(): return lax.ppermute(x, axis, pairs)  39.2 us
  transfers between devices with their start and end apart: 23, of which 21 were waited for; matrix products, arithmetic and copies ran while one was open for 7% of the time, Pallas kernels for 0%

profile of v1, /device:TPU:59, one launch (start us, length us, event | category | flops | bytes accessed | tf_op | source)
XLA Modules:
  0.0 564.0 jit_solution(12720960103317303368)
XLA Ops:
  0.7 2.9 dynamic-slice_bitcast_fusion.1
  10.0 3.1 fusion.8
  13.2 6.1 %collective-permute-done.1 = f32[2,128,512]{2,1,0:T(8,128)} collective-permute-done((f32[2,128,512]{2,1,0:T(8,128)}, f32[2,128,512]{2,1,0:T(8,128)}, u32[]{:S(2)}, u32[]{:S(2)}) %collective-permute-start.1) | collective-permute-done | bytes 524320 | tf_op jit(solution)/shard_map/ppermute | solution.py:11
  25.2 11.7 %cholesky.130 = f32[128,128]{1,0:T(8,128)S(1)} custom-call(f32[128,128]{1,0:T(8,128)S(1)} %cholesky.194), custom_call_target="Cholesky" | custom-call | tf_op jit(solution)/shard_map/jit(cholesky)/cholesky | solution.py:60
  36.9 9.8 %custom-call.26 = f32[1,128,128]{1,2,0:T(8,128)S(1)} custom-call(f32[1,128,128]{2,1,0:T(8,128)S(1)} %get-tuple-element.251), custom_call_target="InvertDiagBlocksLowerTriangular" | custom-call | tf_op jit(solution)/shard_map/jit(cholesky)/cholesky | solution.py:60
  47.3 11.9 %cholesky.147 = f32[128,128]{1,0:T(8,128)S(1)} custom-call(f32[128,128]{1,0:T(8,128)S(1)} %convolution_subtract_fusion.16), custom_call_target="Cholesky" | custom-call | tf_op jit(solution)/shard_map/jit(cholesky)/cholesky | solution.py:60
  61.3 3.8 while.16
  65.1 19.7 %custom-call.22 = f32[2,128,128]{1,2,0:T(8,128)S(1)} custom-call(f32[2,128,128]{2,1,0:T(8,128)S(1)} %get-tuple-element.129), custom_call_target="InvertDiagBlocksLowerTriangular" | custom-call | tf_op jit(solution)/shard_map/jit(_cho_solve)/triangular_solve | solution.py:61
  93.0 26.5 %collective-permute-done.2 = f32[2,384,512]{2,1,0:T(8,128)S(1)} collective-permute-done((f32[2,384,512]{2,1,0:T(8,128)}, f32[2,384,512]{2,1,0:T(8,128)S(1)}, u32[]{:S(2)}, u32[]{:S(2)}) %collective-permute-start.2) | collective-permute-done | bytes 1572896 | tf_op jit(solution)/shard_map/ppermute | solution.py:11
  128.7 13.6 %fusion.91 = f32[384,768]{1,0:T(8,128)S(1)} fusion(f32[128,768]{1,0:T(8,128)S(1)} %fusion.111, f32[2,384,512]{2,1,0:T(8,128)S(1)} %get-tuple-element.228), kind=kOutput, calls=%fused_computation.236 | convolution fusion | flops 452984832 | bytes 1769472 | tf_op jit(solution)/shard_map/dot_general | solution.py:15
  151.3 11.5 %collective-permute-done.3 = f32[2,128,640]{2,1,0:T(8,128)S(1)} collective-permute-done((f32[2,128,640]{2,1,0:T(8,128)S(1)}, f32[2,128,640]{2,1,0:T(8,128)S(1)}, u32[]{:S(2)}, u32[]{:S(2)}) %collective-permute-start.3) | collective-permute-done | bytes 655392 | tf_op jit(solution)/shard_map/ppermute | solution.py:11
  166.6 11.7 %cholesky.164 = f32[128,128]{1,0:T(8,128)S(1)} custom-call(f32[128,128]{1,0:T(8,128)S(1)} %cholesky.197), custom_call_target="Cholesky" | custom-call | tf_op jit(solution)/shard_map/jit(cholesky)/cholesky | solution.py:60
  178.9 9.8 %custom-call.27 = f32[1,128,128]{1,2,0:T(8,128)S(1)} custom-call(f32[1,128,128]{2,1,0:T(8,128)S(1)} %get-tuple-element.247), custom_call_target="InvertDiagBlocksLowerTriangular" | custom-call | tf_op jit(solution)/shard_map/jit(cholesky)/cholesky | solution.py:60
  190.9 11.7 %cholesky.181 = f32[128,128]{1,0:T(8,128)S(1)} custom-call(f32[128,128]{1,0:T(8,128)S(1)} %convolution_subtract_fusion.14), custom_call_target="Cholesky" | custom-call | tf_op jit(solution)/shard_map/jit(cholesky)/cholesky | solution.py:60
  204.6 3.8 while.17
  208.4 20.7 %custom-call.23 = f32[2,128,128]{1,2,0:T(8,128)} custom-call(f32[2,128,128]{2,1,0:T(8,128)S(1)} %get-tuple-element.137), custom_call_target="InvertDiagBlocksLowerTriangular" | custom-call | tf_op jit(solution)/shard_map/jit(_cho_solve)/triangular_solve | solution.py:61
  241.9 44.1 %collective-permute-done.4 = f32[2,512,640]{2,1,0:T(8,128)S(1)} collective-permute-done((f32[2,512,640]{2,1,0:T(8,128)}, f32[2,512,640]{2,1,0:T(8,128)S(1)}, u32[]{:S(2)}, u32[]{:S(2)}) %collective-permute-start.4) | collective-permute-done | bytes 2621472 | tf_op jit(solution)/shard_map/ppermute | solution.py:11
  314.3 3.7 fusion
  318.0 3.7 fusion.1
  321.7 3.7 fusion.24
  325.4 3.9 fusion.22
  332.1 6.5 %collective-permute-done.5 = f32[2,528,512]{2,1,0:T(8,128)S(1)} collective-permute-done((f32[2,528,512]{2,1,0:T(8,128)S(1)}, f32[2,528,512]{2,1,0:T(8,128)S(1)}, u32[]{:S(2)}, u32[]{:S(2)}) %collective-permute-start.5) | collective-permute-done | bytes 2162720 | tf_op jit(solution)/shard_map/ppermute | solution.py:109
  353.3 26.2 %collective-permute-done.6 = f32[2,528,512]{2,1,0:T(8,128)} collective-permute-done((f32[2,528,512]{2,1,0:T(8,128)}, f32[2,528,512]{2,1,0:T(8,128)}, u32[]{:S(2)}, u32[]{:S(2)}) %collective-permute-start.6) | collective-permute-done | bytes 2162720 | tf_op jit(solution)/shard_map/ppermute | solution.py:109
  387.5 3.1 fusion.57
  390.6 3.1 fusion.59
  393.7 3.2 convolution_subtract_fusion.2
  396.9 3.2 fusion.170
  402.5 5.6 copy.14
  408.1 129.9 %while.18 = (s32[]{:T(128)}, f32[16,1024]{1,0:T(8,128)S(1)}, s32[]{:T(128)}, f32[1024,1024]{1,0:T(8,128)}, f32[16,1024]{1,0:T(8,128)S(1)}, /*index=5*/s32[]{:T(128)}, s32[]{:T(128)}, s32[]{:T(128)}, s32[]{:T(128)}, s32[]{:T(128)}) while((s32[]{:T(128)}, f32[16,1024]{1,0:T(8,128)S(1)}, s32[]{:T(128)}, f32[1024,1024]{1,0:T(8,128)}, ...), condition=%wide.region_7.9_spmd.clone, body=%wide.region_4.8_spmd.clone.sunk | while | flops 100728840 | bytes 4980980 | solution.py:228
  408.1 4.9 collective-permute-start
  413.0 3.9 collective-permute-done
  419.6 5.4 collective-permute-done
  427.1 6.1 %collective-permute-done = f32[16,1024]{1,0:T(8,128)S(1)} collective-permute-done((f32[16,1024]{1,0:T(8,128)S(1)}, f32[16,1024]{1,0:T(8,128)S(1)}, u32[]{:S(2)}, u32[]{:S(2)}) %collective-permute-start) | collective-permute-done | bytes 65568 | tf_op jit(solution)/shard_map/while/body/eval_jaxpr/ppermute | solution.py:109
  435.2 6.1 %collective-permute-done = f32[16,1024]{1,0:T(8,128)S(1)} collective-permute-done((f32[16,1024]{1,0:T(8,128)S(1)}, f32[16,1024]{1,0:T(8,128)S(1)}, u32[]{:S(2)}, u32[]{:S(2)}) %collective-permute-start) | collective-permute-done | bytes 65568 | tf_op jit(solution)/shard_map/while/body/eval_jaxpr/ppermute | solution.py:109
  443.4 6.1 %collective-permute-done = f32[16,1024]{1,0:T(8,128)S(1)} collective-permute-done((f32[16,1024]{1,0:T(8,128)S(1)}, f32[16,1024]{1,0:T(8,128)S(1)}, u32[]{:S(2)}, u32[]{:S(2)}) %collective-permute-start) | collective-permute-done | bytes 65568 | tf_op jit(solution)/shard_map/while/body/eval_jaxpr/ppermute | solution.py:109
  451.5 6.1 %collective-permute-done = f32[16,1024]{1,0:T(8,128)S(1)} collective-permute-done((f32[16,1024]{1,0:T(8,128)S(1)}, f32[16,1024]{1,0:T(8,128)S(1)}, u32[]{:S(2)}, u32[]{:S(2)}) %collective-permute-start) | collective-permute-done | bytes 65568 | tf_op jit(solution)/shard_map/while/body/eval_jaxpr/ppermute | solution.py:109
  459.6 6.1 %collective-permute-done = f32[16,1024]{1,0:T(8,128)S(1)} collective-permute-done((f32[16,1024]{1,0:T(8,128)S(1)}, f32[16,1024]{1,0:T(8,128)S(1)}, u32[]{:S(2)}, u32[]{:S(2)}) %collective-permute-start) | collective-permute-done | bytes 65568 | tf_op jit(solution)/shard_map/while/body/eval_jaxpr/ppermute | solution.py:109
  467.7 6.1 %collective-permute-done = f32[16,1024]{1,0:T(8,128)S(1)} collective-permute-done((f32[16,1024]{1,0:T(8,128)S(1)}, f32[16,1024]{1,0:T(8,128)S(1)}, u32[]{:S(2)}, u32[]{:S(2)}) %collective-permute-start) | collective-permute-done | bytes 65568 | tf_op jit(solution)/shard_map/while/body/eval_jaxpr/ppermute | solution.py:109
  475.8 6.1 %collective-permute-done = f32[16,1024]{1,0:T(8,128)S(1)} collective-permute-done((f32[16,1024]{1,0:T(8,128)S(1)}, f32[16,1024]{1,0:T(8,128)S(1)}, u32[]{:S(2)}, u32[]{:S(2)}) %collective-permute-start) | collective-permute-done | bytes 65568 | tf_op jit(solution)/shard_map/while/body/eval_jaxpr/ppermute | solution.py:109
  483.9 6.1 %collective-permute-done = f32[16,1024]{1,0:T(8,128)S(1)} collective-permute-done((f32[16,1024]{1,0:T(8,128)S(1)}, f32[16,1024]{1,0:T(8,128)S(1)}, u32[]{:S(2)}, u32[]{:S(2)}) %collective-permute-start) | collective-permute-done | bytes 65568 | tf_op jit(solution)/shard_map/while/body/eval_jaxpr/ppermute | solution.py:109
  492.1 6.1 %collective-permute-done = f32[16,1024]{1,0:T(8,128)S(1)} collective-permute-done((f32[16,1024]{1,0:T(8,128)S(1)}, f32[16,1024]{1,0:T(8,128)S(1)}, u32[]{:S(2)}, u32[]{:S(2)}) %collective-permute-start) | collective-permute-done | bytes 65568 | tf_op jit(solution)/shard_map/while/body/eval_jaxpr/ppermute | solution.py:109
  500.2 10.1 %collective-permute-done = f32[16,1024]{1,0:T(8,128)S(1)} collective-permute-done((f32[16,1024]{1,0:T(8,128)S(1)}, f32[16,1024]{1,0:T(8,128)S(1)}, u32[]{:S(2)}, u32[]{:S(2)}) %collective-permute-start) | collective-permute-done | bytes 65568 | tf_op jit(solution)/shard_map/while/body/eval_jaxpr/ppermute | solution.py:109
  510.3 3.4 conditional.3
  510.3 3.3 convolution_add_fusion
  515.6 6.1 %collective-permute-done = f32[16,1024]{1,0:T(8,128)S(1)} collective-permute-done((f32[16,1024]{1,0:T(8,128)S(1)}, f32[16,1024]{1,0:T(8,128)S(1)}, u32[]{:S(2)}, u32[]{:S(2)}) %collective-permute-start) | collective-permute-done | bytes 65568 | tf_op jit(solution)/shard_map/while/body/eval_jaxpr/ppermute | solution.py:109
  521.8 3.1 collective-permute-start
  524.9 4.9 collective-permute-done
  531.8 6.1 %collective-permute-done = f32[16,1024]{1,0:T(8,128)S(1)} collective-permute-done((f32[16,1024]{1,0:T(8,128)S(1)}, f32[16,1024]{1,0:T(8,128)S(1)}, u32[]{:S(2)}, u32[]{:S(2)}) %collective-permute-start) | collective-permute-done | bytes 65568 | tf_op jit(solution)/shard_map/while/body/eval_jaxpr/ppermute | solution.py:109
  (382 shorter events, 174.5 us)
Async XLA Ops:
  3.5 4.2 copy-start.12
  6.1 13.1 %collective-permute-start.1 = (f32[2,128,512]{2,1,0:T(8,128)}, f32[2,128,512]{2,1,0:T(8,128)}, u32[]{:S(2)}, u32[]{:S(2)}) collective-permute-start(f32[2,128,512]{2,1,0:T(8,128)} %get-tuple-element.224), channel_id=1, source_target_pairs={{0,1},{1,0},{2,3},{3,2},{4,5},{5,4},{6,7},{7,6},{8,9},{9,8},{10,11... | collective-permute-start | bytes 1572872 | tf_op jit(solution)/shard_map/ppermute | solution.py:11
  10.0 9.2 %copy-start.36 = (f32[2,128,128]{2,1,0:T(8,128)S(1)}, f32[2,128,128]{2,1,0:T(8,128)}, u32[]{:S(2)}) copy-start(f32[2,128,128]{2,1,0:T(8,128)} %get-tuple-element.221) | copy-start | bytes 393220
  10.0 9.2 %copy-start.37 = (f32[2,128,128]{2,1,0:T(8,128)S(1)}, f32[2,128,128]{2,1,0:T(8,128)}, u32[]{:S(2)}) copy-start(f32[2,128,128]{2,1,0:T(8,128)} %get-tuple-element.222) | copy-start | bytes 393220
  20.6 3.9 copy-start.16
  20.7 67.4 %copy-start.21 = (f32[2,128,512]{2,1,0:T(8,128)}, f32[2,128,512]{2,1,0:T(8,128)S(1)}, u32[]{:S(2)}) copy-start(f32[2,128,512]{2,1,0:T(8,128)S(1)} %get-tuple-element.219) | copy-start | bytes 1572868
  24.6 36.6 %copy-start.46 = (s32[2]{0:T(128)S(1)}, s32[2]{0:T(128)}, u32[]{:S(2)}) copy-start(s32[2]{0:T(128)} %iota_multiply_fusion) | copy-start | bytes 28
  65.1 23.0 %copy-start.44 = (s32[2,2]{1,0:T(2,128)}, s32[2,2]{1,0:T(2,128)S(1)}, u32[]{:S(2)}) copy-start(s32[2,2]{1,0:T(2,128)S(1)} %get-tuple-element.431) | copy-start | bytes 52
  84.8 34.7 %collective-permute-start.2 = (f32[2,384,512]{2,1,0:T(8,128)}, f32[2,384,512]{2,1,0:T(8,128)S(1)}, u32[]{:S(2)}, u32[]{:S(2)}) collective-permute-start(f32[2,384,512]{2,1,0:T(8,128)} %fusion.8), channel_id=1, source_target_pairs={{0,1},{1,0},{2,3},{3,2},{4,5},{5,4},{6,7},{7,6},{8,9},{9,8},{10,11... | collective-permute-start | bytes 4718600 | tf_op jit(solution)/shard_map/ppermute | solution.py:11
  89.1 30.3 %copy-start.13 = (f32[2,512,512]{2,1,0:T(8,128)S(1)}, f32[2,512,512]{2,1,0:T(8,128)}, u32[]{:S(2)}) copy-start(f32[2,512,512]{2,1,0:T(8,128)} %copy-done.12) | copy-start | bytes 6291460
  89.2 30.3 %copy-start.22 = (f32[2,128,512]{2,1,0:T(8,128)S(1)}, f32[2,128,512]{2,1,0:T(8,128)}, u32[]{:S(2)}) copy-start(f32[2,128,512]{2,1,0:T(8,128)} %copy-done.21) | copy-start | bytes 1572868
  93.0 27.0 %copy-start.17 = (f32[2,128,512]{2,1,0:T(8,128)S(1)}, f32[2,128,512]{2,1,0:T(8,128)}, u32[]{:S(2)}) copy-start(f32[2,128,512]{2,1,0:T(8,128)} %copy-done.16) | copy-start | bytes 1572868
  147.4 15.5 %collective-permute-start.3 = (f32[2,128,640]{2,1,0:T(8,128)S(1)}, f32[2,128,640]{2,1,0:T(8,128)S(1)}, u32[]{:S(2)}, u32[]{:S(2)}) collective-permute-start(f32[2,128,640]{2,1,0:T(8,128)S(1)} %get-tuple-element.187), channel_id=1, source_target_pairs={{0,2},{1,3},{2,0},{3,1},{4,6},{5,7},{6,4},{7,5},{8,10},{9,11},{10,... | collective-permute-start | bytes 1966088 | tf_op jit(solution)/shard_map/ppermute | solution.py:11
  163.0 71.6 %copy-start.10 = (f32[2,128,640]{2,1,0:T(8,128)}, f32[2,128,640]{2,1,0:T(8,128)S(1)}, u32[]{:S(2)}) copy-start(f32[2,128,640]{2,1,0:T(8,128)S(1)} %get-tuple-element.234) | copy-start | bytes 1966084
  164.3 40.2 %copy-start.41 = (f32[128,128]{0,1:T(8,128)}, f32[128,128]{0,1:T(8,128)S(1)}, u32[]{:S(2)}) copy-start(f32[128,128]{0,1:T(8,128)S(1)} %get-tuple-element.237) | copy-start | bytes 196612
  164.3 40.3 %copy-start.45 = (s32[2,2]{1,0:T(2,128)S(1)}, s32[2,2]{1,0:T(2,128)}, u32[]{:S(2)}) copy-start(s32[2,2]{1,0:T(2,128)} %copy-done.44) | copy-start | bytes 52
  229.1 56.9 %collective-permute-start.4 = (f32[2,512,640]{2,1,0:T(8,128)}, f32[2,512,640]{2,1,0:T(8,128)S(1)}, u32[]{:S(2)}, u32[]{:S(2)}) collective-permute-start(f32[2,512,640]{2,1,0:T(8,128)} %broadcast_select_fusion.4), channel_id=1, source_target_pairs={{0,2},{1,3},{2,0},{3,1},{4,6},{5,7},{6,4},{7,5},{8,10},{9,11},{10,... | collective-permute-start | bytes 7864328 | tf_op jit(solution)/shard_map/ppermute | solution.py:11
  240.0 46.0 %copy-start.24 = (f32[2,128,768]{2,1,0:T(8,128)S(1)}, f32[2,128,768]{2,1,0:T(8,128)}, u32[]{:S(2)}) copy-start(f32[2,128,768]{2,1,0:T(8,128)} %copy-done.23) | copy-start | bytes 2359300
  240.0 46.0 %copy-start.26 = (f32[2,128,768]{2,1,0:T(8,128)S(1)}, f32[2,128,768]{2,1,0:T(8,128)}, u32[]{:S(2)}) copy-start(f32[2,128,768]{2,1,0:T(8,128)} %copy-done.25) | copy-start | bytes 2359300
  240.0 46.0 %copy-start.28 = (f32[2,128,768]{2,1,0:T(8,128)S(1)}, f32[2,128,768]{2,1,0:T(8,128)}, u32[]{:S(2)}) copy-start(f32[2,128,768]{2,1,0:T(8,128)} %copy-done.27) | copy-start | bytes 2359300
  240.0 46.0 %copy-start.30 = (f32[2,128,768]{2,1,0:T(8,128)S(1)}, f32[2,128,768]{2,1,0:T(8,128)}, u32[]{:S(2)}) copy-start(f32[2,128,768]{2,1,0:T(8,128)} %copy-done.29) | copy-start | bytes 2359300
  241.9 44.9 %copy-start.11 = (f32[2,128,640]{2,1,0:T(8,128)S(1)}, f32[2,128,640]{2,1,0:T(8,128)}, u32[]{:S(2)}) copy-start(f32[2,128,640]{2,1,0:T(8,128)} %copy-done.10) | copy-start | bytes 1966084
  312.3 18.5 %copy-start = (f32[2,1024,256]{2,1,0:T(8,128)}, f32[2,1024,256]{2,1,0:T(8,128)S(1)}, u32[]{:S(2)}) copy-start(f32[2,1024,256]{2,1,0:T(8,128)S(1)} %get-tuple-element.196) | copy-start | bytes 6291460
  329.5 9.1 %collective-permute-start.5 = (f32[2,528,512]{2,1,0:T(8,128)S(1)}, f32[2,528,512]{2,1,0:T(8,128)S(1)}, u32[]{:S(2)}, u32[]{:S(2)}) collective-permute-start(f32[2,528,512]{2,1,0:T(8,128)S(1)} %pad_maximum_fusion.5), channel_id=1, source_target_pairs={{0,4},{8,12},{16,20},{24,28},{32,36},{40,44},{48,52},{56,60},{64,6... | collective-permute-start | bytes 6488072 | tf_op jit(solution)/shard_map/ppermute | solution.py:109
  332.1 16.1 %copy-start.2 = (f32[512,512]{1,0:T(8,128)}, f32[512,512]{1,0:T(8,128)S(1)}, u32[]{:S(2)}) copy-start(f32[512,512]{1,0:T(8,128)S(1)} %get-tuple-element.205) | copy-start | bytes 3145732
  338.7 9.5 %copy-start.8 = (f32[2,528,512]{2,1,0:T(8,128)}, f32[2,528,512]{2,1,0:T(8,128)S(1)}, u32[]{:S(2)}) copy-start(f32[2,528,512]{2,1,0:T(8,128)S(1)} %collective-permute-done.5) | copy-start | bytes 6488068
  351.8 27.8 %collective-permute-start.6 = (f32[2,528,512]{2,1,0:T(8,128)}, f32[2,528,512]{2,1,0:T(8,128)}, u32[]{:S(2)}, u32[]{:S(2)}) collective-permute-start(f32[2,528,512]{2,1,0:T(8,128)} %pad_maximum_fusion.6), channel_id=1, source_target_pairs={{4,12},{20,28},{36,44},{52,60},{68,76},{84,92},{100,108},{116,124}... | collective-permute-start | bytes 6488072 | tf_op jit(solution)/shard_map/ppermute | solution.py:109
  353.3 30.7 %copy-start.5 = (f32[512,512]{1,0:T(8,128)S(1)}, f32[512,512]{1,0:T(8,128)}, u32[]{:S(2)}) copy-start(f32[512,512]{1,0:T(8,128)} %copy-done.4) | copy-start | bytes 3145732
  353.3 32.4 %copy-start.7 = (f32[512,512]{1,0:T(8,128)S(1)}, f32[512,512]{1,0:T(8,128)}, u32[]{:S(2)}) copy-start(f32[512,512]{1,0:T(8,128)} %copy-done.6) | copy-start | bytes 3145732
  408.1 8.9 %collective-permute-start = (f32[16,1024]{1,0:T(8,128)S(1)}, f32[16,1024]{1,0:T(8,128)S(1)}, u32[]{:S(2)}, u32[]{:S(2)}) collective-permute-start(f32[16,1024]{1,0:T(8,128)S(1)} %get-tuple-element.414), channel_id=1, source_target_pairs={{12,28},{28,44},{44,60},{60,76},{76,92},{92,108},{108,124},{124,14... | collective-permute-start | bytes 196616 | tf_op jit(solution)/shard_map/while/body/eval_jaxpr/ppermute | solution.py:109
  417.1 8.0 %collective-permute-start = (f32[16,1024]{1,0:T(8,128)S(1)}, f32[16,1024]{1,0:T(8,128)S(1)}, u32[]{:S(2)}, u32[]{:S(2)}) collective-permute-start(f32[16,1024]{1,0:T(8,128)S(1)} %get-tuple-element.414), channel_id=1, source_target_pairs={{12,28},{28,44},{44,60},{60,76},{76,92},{92,108},{108,124},{124,14... | collective-permute-start | bytes 196616 | tf_op jit(solution)/shard_map/while/body/eval_jaxpr/ppermute | solution.py:109
  425.2 8.0 %collective-permute-start = (f32[16,1024]{1,0:T(8,128)S(1)}, f32[16,1024]{1,0:T(8,128)S(1)}, u32[]{:S(2)}, u32[]{:S(2)}) collective-permute-start(f32[16,1024]{1,0:T(8,128)S(1)} %get-tuple-element.414), channel_id=1, source_target_pairs={{12,28},{28,44},{44,60},{60,76},{76,92},{92,108},{108,124},{124,14... | collective-permute-start | bytes 196616 | tf_op jit(solution)/shard_map/while/body/eval_jaxpr/ppermute | solution.py:109
  433.3 8.0 %collective-permute-start = (f32[16,1024]{1,0:T(8,128)S(1)}, f32[16,1024]{1,0:T(8,128)S(1)}, u32[]{:S(2)}, u32[]{:S(2)}) collective-permute-start(f32[16,1024]{1,0:T(8,128)S(1)} %get-tuple-element.414), channel_id=1, source_target_pairs={{12,28},{28,44},{44,60},{60,76},{76,92},{92,108},{108,124},{124,14... | collective-permute-start | bytes 196616 | tf_op jit(solution)/shard_map/while/body/eval_jaxpr/ppermute | solution.py:109
  441.4 8.0 %collective-permute-start = (f32[16,1024]{1,0:T(8,128)S(1)}, f32[16,1024]{1,0:T(8,128)S(1)}, u32[]{:S(2)}, u32[]{:S(2)}) collective-permute-start(f32[16,1024]{1,0:T(8,128)S(1)} %get-tuple-element.414), channel_id=1, source_target_pairs={{12,28},{28,44},{44,60},{60,76},{76,92},{92,108},{108,124},{124,14... | collective-permute-start | bytes 196616 | tf_op jit(solution)/shard_map/while/body/eval_jaxpr/ppermute | solution.py:109
  449.5 8.0 %collective-permute-start = (f32[16,1024]{1,0:T(8,128)S(1)}, f32[16,1024]{1,0:T(8,128)S(1)}, u32[]{:S(2)}, u32[]{:S(2)}) collective-permute-start(f32[16,1024]{1,0:T(8,128)S(1)} %get-tuple-element.414), channel_id=1, source_target_pairs={{12,28},{28,44},{44,60},{60,76},{76,92},{92,108},{108,124},{124,14... | collective-permute-start | bytes 196616 | tf_op jit(solution)/shard_map/while/body/eval_jaxpr/ppermute | solution.py:109
  457.6 8.0 %collective-permute-start = (f32[16,1024]{1,0:T(8,128)S(1)}, f32[16,1024]{1,0:T(8,128)S(1)}, u32[]{:S(2)}, u32[]{:S(2)}) collective-permute-start(f32[16,1024]{1,0:T(8,128)S(1)} %get-tuple-element.414), channel_id=1, source_target_pairs={{12,28},{28,44},{44,60},{60,76},{76,92},{92,108},{108,124},{124,14... | collective-permute-start | bytes 196616 | tf_op jit(solution)/shard_map/while/body/eval_jaxpr/ppermute | solution.py:109
  465.8 8.0 %collective-permute-start = (f32[16,1024]{1,0:T(8,128)S(1)}, f32[16,1024]{1,0:T(8,128)S(1)}, u32[]{:S(2)}, u32[]{:S(2)}) collective-permute-start(f32[16,1024]{1,0:T(8,128)S(1)} %get-tuple-element.414), channel_id=1, source_target_pairs={{12,28},{28,44},{44,60},{60,76},{76,92},{92,108},{108,124},{124,14... | collective-permute-start | bytes 196616 | tf_op jit(solution)/shard_map/while/body/eval_jaxpr/ppermute | solution.py:109
  473.9 8.0 %collective-permute-start = (f32[16,1024]{1,0:T(8,128)S(1)}, f32[16,1024]{1,0:T(8,128)S(1)}, u32[]{:S(2)}, u32[]{:S(2)}) collective-permute-start(f32[16,1024]{1,0:T(8,128)S(1)} %get-tuple-element.414), channel_id=1, source_target_pairs={{12,28},{28,44},{44,60},{60,76},{76,92},{92,108},{108,124},{124,14... | collective-permute-start | bytes 196616 | tf_op jit(solution)/shard_map/while/body/eval_jaxpr/ppermute | solution.py:109
  482.0 8.0 %collective-permute-start = (f32[16,1024]{1,0:T(8,128)S(1)}, f32[16,1024]{1,0:T(8,128)S(1)}, u32[]{:S(2)}, u32[]{:S(2)}) collective-permute-start(f32[16,1024]{1,0:T(8,128)S(1)} %get-tuple-element.414), channel_id=1, source_target_pairs={{12,28},{28,44},{44,60},{60,76},{76,92},{92,108},{108,124},{124,14... | collective-permute-start | bytes 196616 | tf_op jit(solution)/shard_map/while/body/eval_jaxpr/ppermute | solution.py:109
  490.1 8.0 %collective-permute-start = (f32[16,1024]{1,0:T(8,128)S(1)}, f32[16,1024]{1,0:T(8,128)S(1)}, u32[]{:S(2)}, u32[]{:S(2)}) collective-permute-start(f32[16,1024]{1,0:T(8,128)S(1)} %get-tuple-element.414), channel_id=1, source_target_pairs={{12,28},{28,44},{44,60},{60,76},{76,92},{92,108},{108,124},{124,14... | collective-permute-start | bytes 196616 | tf_op jit(solution)/shard_map/while/body/eval_jaxpr/ppermute | solution.py:109
  498.2 12.0 %collective-permute-start = (f32[16,1024]{1,0:T(8,128)S(1)}, f32[16,1024]{1,0:T(8,128)S(1)}, u32[]{:S(2)}, u32[]{:S(2)}) collective-permute-start(f32[16,1024]{1,0:T(8,128)S(1)} %get-tuple-element.414), channel_id=1, source_target_pairs={{12,28},{28,44},{44,60},{60,76},{76,92},{92,108},{108,124},{124,14... | collective-permute-start | bytes 196616 | tf_op jit(solution)/shard_map/while/body/eval_jaxpr/ppermute | solution.py:109
  513.7 8.0 %collective-permute-start = (f32[16,1024]{1,0:T(8,128)S(1)}, f32[16,1024]{1,0:T(8,128)S(1)}, u32[]{:S(2)}, u32[]{:S(2)}) collective-permute-start(f32[16,1024]{1,0:T(8,128)S(1)} %get-tuple-element.414), channel_id=1, source_target_pairs={{12,28},{28,44},{44,60},{60,76},{76,92},{92,108},{108,124},{124,14... | collective-permute-start | bytes 196616 | tf_op jit(solution)/shard_map/while/body/eval_jaxpr/ppermute | solution.py:109
  521.8 8.0 %collective-permute-start = (f32[16,1024]{1,0:T(8,128)S(1)}, f32[16,1024]{1,0:T(8,128)S(1)}, u32[]{:S(2)}, u32[]{:S(2)}) collective-permute-start(f32[16,1024]{1,0:T(8,128)S(1)} %get-tuple-element.414), channel_id=1, source_target_pairs={{12,28},{28,44},{44,60},{60,76},{76,92},{92,108},{108,124},{124,14... | collective-permute-start | bytes 196616 | tf_op jit(solution)/shard_map/while/body/eval_jaxpr/ppermute | solution.py:109
  529.9 8.0 %collective-permute-start = (f32[16,1024]{1,0:T(8,128)S(1)}, f32[16,1024]{1,0:T(8,128)S(1)}, u32[]{:S(2)}, u32[]{:S(2)}) collective-permute-start(f32[16,1024]{1,0:T(8,128)S(1)} %get-tuple-element.414), channel_id=1, source_target_pairs={{12,28},{28,44},{44,60},{60,76},{76,92},{92,108},{108,124},{124,14... | collective-permute-start | bytes 196616 | tf_op jit(solution)/shard_map/while/body/eval_jaxpr/ppermute | solution.py:109
  538.0 12.5 %copy-start.9 = (f32[2,528,512]{2,1,0:T(8,128)S(1)}, f32[2,528,512]{2,1,0:T(8,128)}, u32[]{:S(2)}) copy-start(f32[2,528,512]{2,1,0:T(8,128)} %copy-done.8) | copy-start | bytes 6488068
  538.0 10.2 %collective-permute-start.7 = (f32[2,16,512]{2,1,0:T(8,128)S(1)}, f32[2,16,512]{2,1,0:T(8,128)S(1)}, u32[]{:S(2)}, u32[]{:S(2)}) collective-permute-start(f32[2,16,512]{2,1,0:T(8,128)S(1)} %pad_maximum_fusion.16), channel_id=1, source_target_pairs={{12,4},{28,20},{44,36},{60,52},{76,68},{92,84},{108,100},{124,116}... | collective-permute-start | bytes 196616 | tf_op jit(solution)/shard_map/ppermute | solution.py:109
  549.0 5.4 copy-start.1
  549.0 5.4 collective-permute-start.8
  (22 other events, 51.8 us)
